TPU v7x, 512 devices: a whole 4x4x16 slice. The times are simulated.
512 devices in a mesh: blk: 32 (over z, y_lo), rep: 16 (over x, y_hi, core).
Axes of the slice: x: 4, y: 4 (y_hi: 2, y_lo: 2; y = y_hi * 2 + y_lo), z: 16, core: 2. Of those that a mesh axis runs over, the one named last changes fastest.
Arguments:
- users: bfloat16 [524288, 128], P(('blk', 'rep')), may hold values from -2 to 2
- items: bfloat16 [32768, 128], P('blk'), may hold values from -2 to 2
- ratings: bfloat16 [32, 16, 3, 40, 128, 128], P('blk', 'rep'), may hold values from 0 to 4
- user_tiles: int32 [32, 16, 3, 40], P('blk', 'rep'), may hold values from 0 to 7
- item_tiles: int32 [32, 16, 3, 40], P('blk', 'rep'), may hold values from 0 to 7
- counts: int32 [32, 16, 3], P('blk', 'rep'), may hold values from 5 to 40, as said below
Outputs:
- user_new: bfloat16 [524288, 128], P(('blk', 'rep'))
- item_new: bfloat16 [32768, 128], P('blk')
Inputs may be any that keep to these rules, and one draw needn't show every extreme that they name: `counts`: each device and stop has between 5 and 40 live slots, the first ones of its list; some device has all 40 live for some stop.
All inputs are finite; a program needn't handle non-finite values.
Results may differ from a plain program's by a relative error of at most 0.0033.
Values may be sent and summed in bfloat16 or wider, within the bound.
A program may use at most 64 MiB of HBM per device.

v0:
```python
import math

import jax
import jax.numpy as jnp
from jax import lax
from jax.sharding import PartitionSpec as P

confidence = 0.5
shrinkage = 0.05
step_gain = 0.3
slot_group = 8


def shifted(block, axis, distance):
    devices = range(lax.axis_size(axis))
    route = [((i - distance) % len(devices), i) for i in devices]
    return lax.ppermute(block, axis, route)


def on_device(users, items, ratings, user_tiles, item_tiles, counts):
    tile_size = ratings.shape[-1]
    rank_width = users.shape[1]
    stations = ratings.shape[2]
    slots_all = ratings.shape[3]
    user_count = users.shape[0] // tile_size
    item_count = items.shape[0] // tile_size
    user_blocks = users.reshape(user_count, tile_size, rank_width)
    user_ids = jnp.arange(user_count, dtype=jnp.int32)
    item_ids = jnp.arange(item_count, dtype=jnp.int32)
    group_slots = jnp.arange(slot_group, dtype=jnp.int32)
    grad_user = jnp.zeros((user_count, tile_size, rank_width), jnp.float32)
    current = items
    partials = []
    for station in range(stations):
        if station > 0:
            current = shifted(current, "blk", -1)
        item_blocks = current.reshape(item_count, tile_size, rank_width)
        live_count = counts[0, 0, station]
        groups = (live_count + slot_group - 1) // slot_group
        stop_users = user_tiles[0, 0, station]
        stop_items = item_tiles[0, 0, station]
        stop_ratings = ratings[0, 0, station]

        def group_step(
            group_index,
            totals,
            item_blocks=item_blocks,
            live_count=live_count,
            stop_users=stop_users,
            stop_items=stop_items,
            stop_ratings=stop_ratings,
        ):
            user_acc, item_acc = totals
            first_slot = group_index * slot_group
            user_pick = lax.dynamic_slice_in_dim(stop_users, first_slot, slot_group)
            item_pick = lax.dynamic_slice_in_dim(stop_items, first_slot, slot_group)
            rating_tiles = lax.dynamic_slice_in_dim(stop_ratings, first_slot, slot_group, 0)
            valid_slots = (first_slot + group_slots < live_count).astype(jnp.float32)
            user_rows = user_blocks[user_pick]
            item_rows = item_blocks[item_pick]
            predicted = jnp.einsum(
                "gak,gbk->gab", user_rows, item_rows, preferred_element_type=jnp.float32
            )
            rating_vals = rating_tiles.astype(jnp.float32)
            residual = (
                (1.0 + confidence * rating_vals)
                * (rating_vals - predicted)
                * valid_slots[:, None, None]
            ).astype(jnp.bfloat16)
            user_terms = jnp.einsum(
                "gab,gbk->gak", residual, item_rows, preferred_element_type=jnp.float32
            )
            item_terms = jnp.einsum(
                "gab,gak->gbk", residual, user_rows, preferred_element_type=jnp.float32
            )
            user_onehot = (user_pick[:, None] == user_ids[None, :]).astype(jnp.float32)
            item_onehot = (item_pick[:, None] == item_ids[None, :]).astype(jnp.float32)
            user_acc = user_acc + jnp.einsum(
                "gn,gak->nak", user_onehot, user_terms, precision=lax.Precision.HIGHEST
            )
            item_acc = item_acc + jnp.einsum(
                "gn,gak->nak", item_onehot, item_terms, precision=lax.Precision.HIGHEST
            )
            return (user_acc, item_acc)

        item_zero = jnp.zeros((item_count, tile_size, rank_width), jnp.float32)
        grad_user, item_grad = lax.fori_loop(0, groups, group_step, (grad_user, item_zero))
        partials.append(item_grad.reshape(items.shape[0], rank_width))
    rep_count = lax.axis_size("rep")
    rate_user = step_gain / math.sqrt(stations * slots_all * tile_size * tile_size / users.shape[0])
    rate_item = step_gain / math.sqrt(
        rep_count * stations * slots_all * tile_size * tile_size / items.shape[0]
    )
    users32 = users.astype(jnp.float32)
    items32 = items.astype(jnp.float32)
    user_new = users32 - rate_user * (grad_user.reshape(users.shape) + shrinkage * users32)
    item_sum = jnp.zeros(items.shape, jnp.float32)
    for station in range(stations):
        summed = lax.psum(partials[station], "rep")
        if station > 0:
            summed = shifted(summed, "blk", station)
        item_sum = item_sum + summed
    item_new = (items32 - rate_item * (item_sum + shrinkage * items32)).astype(jnp.bfloat16)
    return (user_new.astype(jnp.bfloat16), item_new)


def solution(mesh):
    return jax.shard_map(
        on_device,
        mesh=mesh,
        in_specs=(
            P(("blk", "rep"), None),
            P("blk", None),
            P("blk", "rep", None, None, None, None),
            P("blk", "rep", None, None),
            P("blk", "rep", None, None),
            P("blk", "rep", None),
        ),
        out_specs=(P(("blk", "rep"), None), P("blk", None)),
        check_vma=False,
    )
```

profile of v0, /device:TPU:8, one launch (start us, length us, event | category | flops | bytes accessed | tf_op | source)
XLA Modules:
  0.0 288.1 jit_solution(16694756250456003882)
XLA Ops:
  7.2 7.7 %collective-permute-start = (bf16[1024,128]{1,0:T(8,128)(2,1)}, bf16[1024,128]{1,0:T(8,128)(2,1)}, u32[]{:S(2)}, u32[]{:S(2)}) collective-permute-start(bf16[1024,128]{1,0:T(8,128)(2,1)} %param.13), channel_id=1, source_target_pairs={{16,0},{32,16},{48,32},{64,48},{80,64},{96,80},{112,96},{128,112},... | collective-permute-start | bytes 786440 | tf_op jit(solution)/shard_map/ppermute | solution.py:17
  14.9 1.4 fusion.48
  17.1 4.1 %slice_bitcast_fusion = (bf16[40,128,128]{2,1,0:T(8,128)(2,1)}, bf16[40,128,128]{2,1,0:T(8,128)(2,1)S(1)}, bf16[40,128,128]{2,1,0:T(8,128)(2,1)}) fusion(bf16[1,1,3,40,128,128]{5,4,3,2,1,0:T(8,128)(2,1)} %param.14), kind=kLoop, calls=%fused_computation.75 | loop fusion | bytes 7864320 | tf_op jit(solution)/shard_map/squeeze | solution.py:42
  21.3 8.5 %while.45 = (s32[]{:T(128)}, f32[8,128,128]{2,0,1:T(8,128)S(1)}, f32[8,128,128]{2,0,1:T(8,128)S(1)}, s32[]{:T(128)}, s32[40]{0:T(128)S(1)}, /*index=5*/bf16[40,1...) while((s32[]{:T(128)}, f32[8,128,128]{2,0,1:T(8,128)S(1)}, ...), condition=%wide.region_1.2_spmd.clone.clone, body=%wide.region_0.1_spmd.clone.clone.sunk | while | flops 127011024 | bytes 7348867 | solution.py:87
  23.9 0.7 convolution_add_fusion.13
  24.8 0.7 convolution_add_fusion.12
  28.2 0.7 convolution_add_fusion.13
  29.1 0.7 convolution_add_fusion.12
  31.1 0.9 copy.9
  32.0 7.1 %collective-permute-start.1 = (bf16[1024,128]{1,0:T(8,128)(2,1)}, bf16[1024,128]{1,0:T(8,128)(2,1)S(1)}, u32[]{:S(2)}, u32[]{:S(2)}) collective-permute-start(bf16[1024,128]{1,0:T(8,128)(2,1)} %collective-permute-done), channel_id=1, source_target_pairs={{16,0},{32,16},{48,32},{64,48},{80,64},{96,80},{112,96},{128,112},... | collective-permute-start | bytes 786440 | tf_op jit(solution)/shard_map/ppermute | solution.py:17
  39.1 30.3 %while.46 = (s32[]{:T(128)}, f32[8,128,128]{2,0,1:T(8,128)S(1)}, f32[8,128,128]{2,0,1:T(8,128)S(1)}, s32[]{:T(128)}, s32[40]{0:T(128)S(1)}, /*index=5*/bf16[40,1...) while((s32[]{:T(128)}, f32[8,128,128]{2,0,1:T(8,128)S(1)}, ...), condition=%wide.region_3.4_spmd.clone.clone, body=%wide.region_2.3_spmd.clone.clone.sunk | while | flops 127011024 | bytes 7348867 | solution.py:87
  39.9 1.5 gather_fusion.3
  42.0 1.3 fusion.135
  43.5 0.7 convolution_add_fusion.15
  44.5 0.7 convolution_add_fusion.14
  45.9 1.5 gather_fusion.3
  48.0 1.3 fusion.135
  49.6 0.7 convolution_add_fusion.15
  50.5 0.7 convolution_add_fusion.14
  52.0 1.5 gather_fusion.3
  54.1 1.3 fusion.135
  55.7 0.7 convolution_add_fusion.15
  56.6 0.7 convolution_add_fusion.14
  58.0 1.5 gather_fusion.3
  60.2 1.3 fusion.135
  61.7 0.7 convolution_add_fusion.15
  62.6 0.7 convolution_add_fusion.14
  64.1 1.5 gather_fusion.3
  66.2 1.3 fusion.135
  67.8 0.7 convolution_add_fusion.15
  68.7 0.7 convolution_add_fusion.14
  69.4 0.9 copy.10
  70.4 10.5 %while.47 = (s32[]{:T(128)}, f32[8,128,128]{2,0,1:T(8,128)S(1)}, f32[8,128,128]{2,0,1:T(8,128)S(1)}, s32[]{:T(128)}, s32[40]{0:T(128)S(1)}, /*index=5*/bf16[40,1...) while((s32[]{:T(128)}, f32[8,128,128]{2,0,1:T(8,128)S(1)}, ...), condition=%wide.region_5.6_spmd.clone.clone, body=%wide.region_4.5_spmd.clone.clone.sunk | while | flops 127011024 | bytes 7348867 | solution.py:87
  71.7 0.7 compare_convert_fusion.8
  72.4 1.3 fusion.148
  74.0 0.7 convolution_add_fusion.17
  74.9 0.7 convolution_add_fusion.16
  77.7 1.3 fusion.148
  79.2 0.7 convolution_add_fusion.17
  80.2 0.7 convolution_add_fusion.16
  80.9 0.9 copy.11
  81.8 170.0 %all-reduce.3.cloned.1.call-done = (f32[1024,128]{1,0:T(8,128)}, f32[1024,128]{1,0:T(8,128)}, f32[1024,128]{1,0:T(8,128)}) async-done(((f32[1024,128]{1,0:T(8,128)}, f32[1024,128]{1,0:T(8,128)}, f32[1024,128]{1,0:T(8,128)}), (f32[1024,128]{1,0:T(8,128)}, f32[1024,128]{1,0:T(8,128)}, f32[1024,128]{1,0:T(8,128)})) %all-reduce.3.cloned.1.call-update) | async-done | bytes 1572880 | tf_op jit(solution)/shard_map/psum | solution.py:99
  251.8 4.1 %collective-permute-start.2 = (f32[1024,128]{1,0:T(8,128)}, f32[1024,128]{1,0:T(8,128)S(1)}, u32[]{:S(2)}, u32[]{:S(2)}) collective-permute-start(f32[1024,128]{1,0:T(8,128)} %get-tuple-element.514), channel_id=1, source_target_pairs={{496,0},{0,16},{16,32},{32,48},{48,64},{64,80},{80,96},{96,112},{1... | collective-permute-start | bytes 1572872 | tf_op jit(solution)/shard_map/ppermute | solution.py:17
  255.9 3.5 %collective-permute-start.3 = (f32[1024,128]{1,0:T(8,128)}, f32[1024,128]{1,0:T(8,128)S(1)}, u32[]{:S(2)}, u32[]{:S(2)}) collective-permute-start(f32[1024,128]{1,0:T(8,128)} %get-tuple-element.512), channel_id=1, source_target_pairs={{480,0},{496,16},{0,32},{16,48},{32,64},{48,80},{64,96},{80,112},{... | collective-permute-start | bytes 1572872 | tf_op jit(solution)/shard_map/ppermute | solution.py:17
  259.5 0.8 fusion.44
  260.3 8.2 %collective-permute-done.2 = f32[1024,128]{1,0:T(8,128)S(1)} collective-permute-done((f32[1024,128]{1,0:T(8,128)}, f32[1024,128]{1,0:T(8,128)S(1)}, u32[]{:S(2)}, u32[]{:S(2)}) %collective-permute-start.2) | collective-permute-done | bytes 524320 | tf_op jit(solution)/shard_map/ppermute | solution.py:17
  268.5 11.9 %collective-permute-done.3 = f32[1024,128]{1,0:T(8,128)S(1)} collective-permute-done((f32[1024,128]{1,0:T(8,128)}, f32[1024,128]{1,0:T(8,128)S(1)}, u32[]{:S(2)}, u32[]{:S(2)}) %collective-permute-start.3) | collective-permute-done | bytes 524320 | tf_op jit(solution)/shard_map/ppermute | solution.py:17
  280.4 0.8 fusion.47
  (88 shorter events, 18.7 us)
Async XLA Ops:
  7.2 244.6 %all-reduce.3.cloned.1.call-start = ((), (), s32[]{:S(2)}) async-start(), calls=%async_computation | async-start | bytes 3145728 | tf_op jit(solution)/shard_map/psum | solution.py:99
  7.2 24.8 %collective-permute-start = (bf16[1024,128]{1,0:T(8,128)(2,1)}, bf16[1024,128]{1,0:T(8,128)(2,1)}, u32[]{:S(2)}, u32[]{:S(2)}) collective-permute-start(bf16[1024,128]{1,0:T(8,128)(2,1)} %param.13), channel_id=1, source_target_pairs={{16,0},{32,16},{48,32},{64,48},{80,64},{96,80},{112,96},{128,112},... | collective-permute-start | bytes 786440 | tf_op jit(solution)/shard_map/ppermute | solution.py:17
  17.0 4.2 %copy-start.3 = (s32[1,1,3,40]{3,1,2,0:T(1,128)S(1)}, s32[1,1,3,40]{3,1,2,0:T(1,128)}, u32[]{:S(2)}) copy-start(s32[1,1,3,40]{3,1,2,0:T(1,128)} %param.16) | copy-start | bytes 1444
  17.0 4.2 %copy-start.4 = (s32[1,1,3,40]{3,1,2,0:T(1,128)S(1)}, s32[1,1,3,40]{3,1,2,0:T(1,128)}, u32[]{:S(2)}) copy-start(s32[1,1,3,40]{3,1,2,0:T(1,128)} %param.15) | copy-start | bytes 1444
  17.0 4.2 %copy-start = (bf16[1024,128]{1,0:T(8,128)(2,1)S(1)}, bf16[1024,128]{1,0:T(8,128)(2,1)}, u32[]{:S(2)}) copy-start(bf16[1024,128]{1,0:T(8,128)(2,1)} %param.12) | copy-start | bytes 786436
  17.1 4.2 %copy-start.1 = (bf16[1024,128]{1,0:T(8,128)(2,1)S(1)}, bf16[1024,128]{1,0:T(8,128)(2,1)}, u32[]{:S(2)}) copy-start(bf16[1024,128]{1,0:T(8,128)(2,1)} %param.13) | copy-start | bytes 786436
  32.0 38.3 %collective-permute-start.1 = (bf16[1024,128]{1,0:T(8,128)(2,1)}, bf16[1024,128]{1,0:T(8,128)(2,1)S(1)}, u32[]{:S(2)}, u32[]{:S(2)}) collective-permute-start(bf16[1024,128]{1,0:T(8,128)(2,1)} %collective-permute-done), channel_id=1, source_target_pairs={{16,0},{32,16},{48,32},{64,48},{80,64},{96,80},{112,96},{128,112},... | collective-permute-start | bytes 786440 | tf_op jit(solution)/shard_map/ppermute | solution.py:17
  251.8 28.6 %copy-start.2 = (f32[1024,128]{1,0:T(8,128)S(1)}, f32[1024,128]{1,0:T(8,128)}, u32[]{:S(2)}) copy-start(f32[1024,128]{1,0:T(8,128)} %get-tuple-element.513) | copy-start | bytes 1572868
  251.8 16.7 %collective-permute-start.2 = (f32[1024,128]{1,0:T(8,128)}, f32[1024,128]{1,0:T(8,128)S(1)}, u32[]{:S(2)}, u32[]{:S(2)}) collective-permute-start(f32[1024,128]{1,0:T(8,128)} %get-tuple-element.514), channel_id=1, source_target_pairs={{496,0},{0,16},{16,32},{32,48},{48,64},{64,80},{80,96},{96,112},{1... | collective-permute-start | bytes 1572872 | tf_op jit(solution)/shard_map/ppermute | solution.py:17
  255.9 24.5 %collective-permute-start.3 = (f32[1024,128]{1,0:T(8,128)}, f32[1024,128]{1,0:T(8,128)S(1)}, u32[]{:S(2)}, u32[]{:S(2)}) collective-permute-start(f32[1024,128]{1,0:T(8,128)} %get-tuple-element.512), channel_id=1, source_target_pairs={{480,0},{496,16},{0,32},{16,48},{32,64},{48,80},{64,96},{80,112},{... | collective-permute-start | bytes 1572872 | tf_op jit(solution)/shard_map/ppermute | solution.py:17
Sparse Core Ops, SparseCore 0:
  81.9 169.7 all-reduce.2
where the time goes:
time: 292 us; the launch traced here: 288 us
  waiting for transfers between devices  190 us (65%)
  matrix products  26.8 us (9%)
  local copies, waits for them, and re-layouts  24 us (8%)
  starting transfers between devices  22.4 us (8%)
  between operations  16.1 us (6%)
  other arithmetic  7.93 us (3%)
    psum x1, waiting for transfers between devices, on_device(): summed = lax.psum(partials[station], 'rep')  170 us
    ppermute x4, starting transfers between devices, shifted(): return lax.ppermute(block, axis, route)  22.4 us
    ppermute x4, waiting for transfers between devices, shifted(): return lax.ppermute(block, axis, route)  20.1 us
    gather x9, local copies, waits for them, and re-layouts, group_step(): item_rows = item_blocks[item_pick]  10.1 us
    dot_general x9, matrix products, group_step(): jnp.einsum('gak,gbk->gab', user_rows, item_rows, preferred_element_type=j...  9.52 us
    dot_general x9, matrix products, group_step(): jnp.einsum('gn,gak->nak', user_onehot, user_terms, precision=lax.Precisio...  6.42 us
    dot_general x9, matrix products, group_step(): jnp.einsum('gn,gak->nak', item_onehot, item_terms, precision=lax.Precisio...  6.41 us
  transfers between devices with their start and end apart: 5, of which 3 were waited for; matrix products, arithmetic and copies ran while one was open for 16% of the time, Pallas kernels for 0%

commit v1 on v0

v1 whole, which is shorter than its diff:
```python
import functools
import math

import jax
import jax.numpy as jnp
from jax import lax
from jax.experimental import pallas as pl
from jax.experimental.pallas import tpu as pltpu
from jax.sharding import PartitionSpec as P

CONFIDENCE = 0.5
SHRINKAGE = 0.05
STEP_GAIN = 0.3
GROUP = 20
MESH = pl.DeviceIdType.MESH
F32 = jnp.float32
BF16 = jnp.bfloat16
ORDER = (0, 2, 1)


def kernel(
    rate_user,
    rate_item,
    tab,
    users_hbm,
    items_hbm,
    ratings_hbm,
    user_out,
    item_out,
    users,
    block_0,
    block_1,
    block_2,
    flipped,
    rbuf,
    sums_user,
    sums_item,
    half_out,
    half_in,
    chip_sum,
    pieces,
    fwd_out,
    fwd_in,
    unew,
    inew,
    load_sem,
    fetch_sem,
    swap_sem,
    half_sem,
    piece_sem,
    fwd_sem,
    gather_sem,
    pair_sem,
    out_sem,
):
    blocks = (block_0, block_1, block_2)
    nblk = lax.axis_size("blk")
    nrep = lax.axis_size("rep")
    nq = nrep // 2
    tiles, tile, _ = users.shape
    slots = rbuf.shape[1]
    half = tile // 2
    per = tiles // nq
    quarter = tiles // 4
    b = lax.axis_index("blk")
    r = lax.axis_index("rep")
    yl = b % 2
    q = r // 2
    c = r % 2
    yh = q % 2

    def col(distance):
        return (b + nblk + distance) % nblk

    partner = (b, r + 1 - 2 * c)
    near = b + 1 - 2 * yl
    same = (near, r)
    other = (near, r + 2 - 4 * yh)

    def rating_load(s):
        return pltpu.make_async_copy(ratings_hbm.at[s], rbuf.at[s], load_sem.at[s])

    user_load = pltpu.make_async_copy(users_hbm, users, load_sem.at[3])
    item_load = pltpu.make_async_copy(items_hbm, block_0, load_sem.at[4])
    user_load.start()
    item_load.start()
    for s in ORDER:
        rating_load(s).start()

    barrier = pltpu.get_barrier_semaphore()
    friends = [partner, (col(-2), r), (col(2), r), (col(-1), r), (col(1), r), other]
    friends += [(b, 2 * ((q + d) % nq) + c) for d in range(1, nq)]
    for friend in friends:
        pl.semaphore_signal(barrier, inc=1, device_id=friend, device_id_type=MESH)
    zero = jnp.zeros((tile, tile), F32)
    for s in range(3):
        sums_user[s, slots] = zero
        sums_item[s, slots] = zero
    pl.semaphore_wait(barrier, len(friends))

    def remote(src, dst, sems, i, target):
        return pltpu.make_async_remote_copy(
            src_ref=src,
            dst_ref=dst,
            send_sem=sems.at[0, i],
            recv_sem=sems.at[1, i],
            device_id=target,
            device_id_type=MESH,
        )

    def part(h):
        return pl.ds((2 * c + h) * quarter, quarter)

    def far_copy(h):
        return remote(items_hbm.at[part(h)], block_2.at[part(h)], fetch_sem, h, (col(-2), r))

    def near_copy(h, src):
        return remote(src, block_1.at[part(h)], fetch_sem, 2 + h, other if h else same)

    def swap_copy(s, h):
        view = blocks[s].at[part(h)]
        return remote(view, view, swap_sem, 2 * (s - 1) + h, partner)

    for h in range(2):
        far_copy(h).start()

    @pl.when(yl == 1)
    def _():
        for h in range(2):
            near_copy(h, items_hbm.at[part(h)]).start()

    def compute(s):
        for t in range(tiles):
            flipped[t] = blocks[s][t].T
        count = tab[s, 0, 2 * slots + tiles]

        def body(i, carry):
            base = i * GROUP
            held = []
            for g in range(GROUP):
                k = base + g
                u = users[tab[s, 0, k]]
                it = tab[s, 1, k]
                v = blocks[s][it]
                p = jnp.dot(u, flipped[it], preferred_element_type=F32)
                rating = rbuf[s, k].astype(F32)
                live = (k < count).astype(F32)
                e = ((1.0 + CONFIDENCE * rating) * (rating - p) * live).astype(BF16)
                held.append((k, u, v, e))
            for k, u, v, e in held:
                gu = jnp.dot(e, v, preferred_element_type=F32)
                gi = lax.dot_general(e, u, (((0,), (0,)), ((), ())), preferred_element_type=F32)
                sums_user[s, k] = gu + sums_user[s, tab[s, 0, slots + k]]
                sums_item[s, k] = gi + sums_item[s, tab[s, 1, slots + k]]
            return carry

        lax.fori_loop(0, slots // GROUP, body, 0)

    def half_copy(s):
        return remote(half_out.at[s], half_in.at[s], half_sem, s, partner)

    def send_half(s):
        for t in range(tiles):
            last = tab[s, 1, 2 * slots + t]
            rows = pl.ds(pl.multiple_of((1 - c) * half, half), half)
            half_out[s, t] = sums_item[s, last, rows].astype(BF16)
        half_copy(s).start()

    def piece_copy(s, d):
        target = (q + d) % nq
        return remote(
            chip_sum.at[s, pl.ds(target * per, per)],
            pieces.at[s, d - 1],
            piece_sem,
            s * (nq - 1) + d - 1,
            (b, 2 * target + c),
        )

    def send_pieces(s):
        half_copy(s).wait_recv()
        for t in range(tiles):
            last = tab[s, 1, 2 * slots + t]
            rows = pl.ds(pl.multiple_of(c * half, half), half)
            both = sums_item[s, last, rows] + half_in[s, t].astype(F32)
            chip_sum[s, t] = both.astype(BF16)
        for d in sorted(range(1, nq), key=lambda d: abs(d - nq // 2)):
            piece_copy(s, d).start()

    def column_sum(s):
        for d in range(1, nq):
            piece_copy(s, d).wait_recv()
        total = chip_sum[s, pl.ds(q * per, per)].astype(F32)
        for d in range(1, nq):
            total = total + pieces[s, d - 1].astype(F32)
        return total

    def fwd_copy(s):
        return remote(fwd_out.at[s - 1], fwd_in.at[s - 1], fwd_sem, s - 1, (col(s), r))

    user_load.wait()
    item_load.wait()
    rating_load(0).wait()
    compute(0)
    send_half(0)

    for h in range(2):
        far_copy(h).wait_recv()
        swap_copy(2, h).start()

        @pl.when(yl == 0)
        def _():
            near_copy(h, block_2.at[part(h)]).start()

    send_pieces(0)
    for h in range(2):
        swap_copy(2, h).wait_recv()
    rating_load(2).wait()
    compute(2)
    send_half(2)

    for h in range(2):
        near_copy(h, items_hbm.at[part(h)]).wait_recv()
        swap_copy(1, h).start()
    send_pieces(2)
    for h in range(2):
        swap_copy(1, h).wait_recv()
    rating_load(1).wait()
    compute(1)
    send_half(1)

    for t in range(tiles):
        grad = zero
        for s in ORDER:
            grad = grad + sums_user[s, tab[s, 0, 2 * slots + t]]
        old = users[t].astype(F32)
        unew[t] = (old - rate_user * (grad + SHRINKAGE * old)).astype(BF16)
    user_store = pltpu.make_async_copy(unew, user_out, out_sem.at[0])
    user_store.start()

    send_pieces(1)
    total = column_sum(0)
    for s in (2, 1):
        fwd_out[s - 1] = column_sum(s)
        fwd_copy(s).start()
    for s in (2, 1):
        fwd_copy(s).wait_recv()
        total = total + fwd_in[s - 1]

    mine = pl.ds(q * per, per)
    old = block_0[mine, pl.ds(pl.multiple_of(c * half, half), half)].astype(F32)
    inew[mine, c] = (old - rate_item * (total + SHRINKAGE * old)).astype(BF16)

    def gather_copy(d):
        return remote(
            inew.at[mine, c],
            inew.at[mine, c],
            gather_sem,
            d - 1,
            (b, 2 * ((q + d) % nq) + c),
        )

    def gathered(d):
        view = inew.at[pl.ds(((q + nq - d) % nq) * per, per), c]
        return remote(view, view, gather_sem, d - 1, (b, 2 * ((q + d) % nq) + c))

    def pair_copy(d):
        view = inew.at[pl.ds(((q + nq - d) % nq) * per, per), c]
        return remote(view, view, pair_sem, d, partner)

    def paired(d):
        view = inew.at[pl.ds(((q + nq - d) % nq) * per, per), 1 - c]
        return remote(view, view, pair_sem, d, partner)

    order = sorted(range(1, nq), key=lambda d: abs(d - nq // 2))
    for d in order:
        gather_copy(d).start()
    pair_copy(0).start()
    for d in reversed(order):
        gathered(d).wait_recv()
        pair_copy(d).start()
    for d in range(nq):
        paired(d).wait_recv()
    item_store = pltpu.make_async_copy(inew, item_out, out_sem.at[1])
    item_store.start()

    for h in range(2):
        far_copy(h).wait_send()
        near_copy(h, items_hbm.at[part(h)]).wait_send()
        for s in (1, 2):
            swap_copy(s, h).wait_send()
    for s in ORDER:
        half_copy(s).wait_send()
        for d in range(1, nq):
            piece_copy(s, d).wait_send()
    for s in (1, 2):
        fwd_copy(s).wait_send()
    for d in range(1, nq):
        gather_copy(d).wait_send()
    for d in range(nq):
        pair_copy(d).wait_send()
    user_store.wait()
    item_store.wait()


def slot_table(user_tiles, item_tiles, counts, tiles):
    picks = jnp.stack([user_tiles, item_tiles], axis=1)
    stops, _, slots = picks.shape
    ids = jnp.arange(slots, dtype=jnp.int32)
    every = jnp.broadcast_to(jnp.arange(tiles, dtype=jnp.int32), (stops, 2, tiles))
    wanted = jnp.concatenate([picks, every], axis=2)
    limit = jnp.concatenate([ids, jnp.full((tiles,), slots, jnp.int32)])
    fits = (wanted[..., :, None] == picks[..., None, :]) & (ids[None, :] < limit[:, None])
    found = jnp.max(jnp.where(fits, ids, -1), axis=3)
    found = jnp.where(found < 0, slots, found)
    tail = jnp.broadcast_to(counts[:, None, None], (stops, 2, 1))
    return jnp.concatenate([picks, found, tail], axis=2)


def on_device(users, items, ratings, user_tiles, item_tiles, counts):
    tile = ratings.shape[-1]
    rank = users.shape[1]
    stops, slots = ratings.shape[2:4]
    tiles = users.shape[0] // tile
    half = tile // 2
    nq = lax.axis_size("rep") // 2
    per = tiles // nq
    rate_user = STEP_GAIN / math.sqrt(stops * slots * tile * tile / users.shape[0])
    rate_item = STEP_GAIN / math.sqrt(2 * nq * stops * slots * tile * tile / items.shape[0])
    table = slot_table(user_tiles[0, 0], item_tiles[0, 0], counts[0, 0], tiles)
    anywhere = pl.BlockSpec(memory_space=pl.ANY)
    dma = pltpu.SemaphoreType.DMA
    user_new, item_new = pl.pallas_call(
        functools.partial(kernel, rate_user, rate_item),
        out_shape=(
            jax.ShapeDtypeStruct((tiles, tile, rank), BF16),
            jax.ShapeDtypeStruct((tiles, 2, half, rank), BF16),
        ),
        in_specs=[pl.BlockSpec(memory_space=pltpu.SMEM), anywhere, anywhere, anywhere],
        out_specs=(anywhere, anywhere),
        scratch_shapes=[
            pltpu.VMEM((tiles, tile, rank), BF16),
            pltpu.VMEM((tiles, tile, rank), BF16),
            pltpu.VMEM((tiles, tile, rank), BF16),
            pltpu.VMEM((tiles, tile, rank), BF16),
            pltpu.VMEM((tiles, rank, tile), BF16),
            pltpu.VMEM((stops, slots, tile, tile), BF16),
            pltpu.VMEM((stops, slots + 1, tile, rank), F32),
            pltpu.VMEM((stops, slots + 1, tile, rank), F32),
            pltpu.VMEM((stops, tiles, half, rank), BF16),
            pltpu.VMEM((stops, tiles, half, rank), BF16),
            pltpu.VMEM((stops, tiles, half, rank), BF16),
            pltpu.VMEM((stops, nq - 1, per, half, rank), BF16),
            pltpu.VMEM((2, per, half, rank), F32),
            pltpu.VMEM((2, per, half, rank), F32),
            pltpu.VMEM((tiles, tile, rank), BF16),
            pltpu.VMEM((tiles, 2, half, rank), BF16),
            dma((5,)),
            dma((2, 4)),
            dma((2, 4)),
            dma((2, 3)),
            dma((2, 3 * (nq - 1))),
            dma((2, 2)),
            dma((2, nq - 1)),
            dma((2, nq)),
            dma((2,)),
        ],
        compiler_params=pltpu.CompilerParams(
            collective_id=0, has_side_effects=True, vmem_limit_bytes=67043328
        ),
    )(
        table,
        users.reshape(tiles, tile, rank),
        items.reshape(tiles, tile, rank),
        ratings[0, 0],
    )
    return user_new.reshape(users.shape), item_new.reshape(items.shape)


def solution(mesh):
    return jax.shard_map(
        on_device,
        mesh=mesh,
        in_specs=(
            P(("blk", "rep"), None),
            P("blk", None),
            P("blk", "rep", None, None, None, None),
            P("blk", "rep", None, None),
            P("blk", "rep", None, None),
            P("blk", "rep", None),
        ),
        out_specs=(P(("blk", "rep"), None), P("blk", None)),
        check_vma=False,
    )
```

time: 292 us -> 53.8 us (0.18)
  the two profiles are of different devices: /device:TPU:8 before, /device:TPU:1 now
where the time goes in v1:
time: 53.8 us; the launch traced here: 53.5 us
  Pallas kernels  45.1 us (84%)
  local copies, waits for them, and re-layouts  4.07 us (8%)
  other arithmetic  3.63 us (7%)
  between operations  0.65 us (1%)
    pallas_call x1, Pallas kernels, on_device(): pl.pallas_call(functools.partial(kernel, rate_user, rate_item), out_shape...  45.1 us
    unnamed x2, local copies, waits for them, and re-layouts  3.34 us
    concatenate x1, other arithmetic, slot_table(): return jnp.concatenate([picks, found, tail], axis=2)  1.36 us

profile of v1, /device:TPU:1, one launch (start us, length us, event | category | flops | bytes accessed | tf_op | source)
XLA Modules:
  0.0 53.5 jit_solution(18040073658977207196)
XLA Ops:
  0.6 0.7 %pad_add_fusion = s32[3,2,40]{2,1,0:T(2,128)S(1)} fusion(s32[3,1,40]{2,1,0:T(1,128)} %bitcast.13, s32[3,1,40]{2,1,0:T(1,128)} %bitcast.16), kind=kLoop, calls=%fused_computation.3 | loop fusion | flops 240 | bytes 1920 | tf_op jit(solution)/shard_map/stack | solution.py:306
  1.3 0.7 %broadcast_in_dim.32 = s32[3,2,1]{2,1,0:T(2,128)S(1)} broadcast(s32[3]{0:T(128)} %bitcast.19), dimensions={0} | broadcast | bytes 36 | tf_op jit(solution)/shard_map/broadcast_in_dim | solution.py:315
  2.1 0.8 %pad_add_fusion.1 = s32[3,2,48]{2,1,0:T(2,128)S(1)} fusion(s32[3,2,8]{2,1,0:T(2,128)S(1)} %broadcast_in_dim.27, s32[3,1,40]{2,1,0:T(1,128)} %bitcast.14, s32[3,1,40]{2,1,0:T(1,128)} %bitcast.17), kind=kLoop, calls=%fused_computation.4 | loop fusion | flops 576 | bytes 2304 | tf_op jit(solution)/shard_map/concatenate | solution.py:310
  2.8 0.7 %iota_compare_fusion = pred[48,40]{0,1:T(8,128)(4,1)S(1)} fusion(s32[48]{0:T(128)} %constant.1.clone.1), kind=kLoop, calls=%fused_computation.1 | loop fusion | flops 1920 | bytes 2112 | tf_op jit(solution)/shard_map/lt | solution.py:312
  3.5 0.1 select_reduce_fusion
  3.6 1.4 %pad_add_fusion.2.tab = s32[3,2,89]{2,1,0:T(2,128)} fusion(s32[3,2,1]{2,1,0:T(2,128)S(1)} %broadcast_in_dim.32, s32[3,2,48]{2,1,0:T(2,128)S(1)} %compare_select_fusion, s32[3,1,40]{2,1,0:T(1,128)} %bitcast.15, s32[3,1,40]{2,1,0:T(1,128)} %bitcast.18), kind=kLoop, calls=%fused_computation.5 | loop fusion | flops 1602 | bytes 4272 | tf_op jit(solution)/shard_map/concatenate | solution.py:316
  5.0 45.1 %shard_map.77 = (bf16[8,128,128]{2,1,0:T(8,128)(2,1)}, bf16[8,2,64,128]{3,2,1,0:T(8,128)(2,1)}) custom-call(s32[3,2,89]{2,1,0:T(2,128)} %pad_add_fusion.2.tab, bf16[8,128,128]{2,1,0:T(8,128)(2,1)} %bitcast.9, bf16[8,128,128]{2,1,0:T(8,128)(2,1)} %bitcast.10, bf16[3,40,128,128]{3,2,1,0:T(8,128)(2,1)} %bitcast.8), custom_call_target="tpu_custom_call" | custom-call | tf_op jit(solution)/shard_map/pallas_call | solution.py:332
  50.1 1.7 %copy.10 = bf16[1024,128]{1,0:T(8,128)(2,1)} copy(bf16[1024,128]{1,0:T(8,128)(2,1)} %bitcast.12) | data formatting | bytes 524288
  51.8 1.7 %copy.11 = bf16[1024,128]{1,0:T(8,128)(2,1)} copy(bf16[1024,128]{1,0:T(8,128)(2,1)} %bitcast.11) | data formatting | bytes 524288
  (2 shorter events, 0.0 us)

commit v2 on v1

v2 whole, which is shorter than its diff:
```python
import functools
import math

import jax
import jax.numpy as jnp
from jax import lax
from jax.experimental import pallas as pl
from jax.experimental.pallas import tpu as pltpu
from jax.sharding import PartitionSpec as P

CONFIDENCE = 0.5
SHRINKAGE = 0.05
STEP_GAIN = 0.3
GROUP = 20
MESH = pl.DeviceIdType.MESH
F32 = jnp.float32
BF16 = jnp.bfloat16
ORDER = (0, 2, 1)


def kernel(
    rate_user,
    rate_item,
    user_tiles_hbm,
    item_tiles_hbm,
    counts_hbm,
    users_hbm,
    items_hbm,
    ratings_hbm,
    user_out,
    item_out,
    users,
    block_0,
    block_1,
    block_2,
    flipped,
    rbuf,
    sums_user,
    sums_item,
    half_out,
    half_in,
    chip_sum,
    pieces,
    fwd_out,
    fwd_in,
    unew,
    inew,
    user_tiles,
    item_tiles,
    counts,
    prev,
    last,
    load_sem,
    fetch_sem,
    swap_sem,
    half_sem,
    piece_sem,
    fwd_sem,
    gather_sem,
    pair_sem,
    out_sem,
):
    blocks = (block_0, block_1, block_2)
    nblk = lax.axis_size("blk")
    nrep = lax.axis_size("rep")
    nq = nrep // 2
    tiles, tile, _ = users.shape
    slots = rbuf.shape[1]
    half = tile // 2
    per = tiles // nq
    quarter = tiles // 4
    b = lax.axis_index("blk")
    r = lax.axis_index("rep")
    yl = b % 2
    q = r // 2
    c = r % 2
    yh = q % 2
    x = q // 2
    nx = nq // 2

    def col(distance):
        return (b + nblk + distance) % nblk

    def target(e):
        return 2 * ((x + e // 2) % nx) + (yh + e) % 2

    def source(e):
        return 2 * ((x + nx - e // 2) % nx) + (yh + e) % 2

    by_distance = sorted(range(1, nq), key=lambda e: (-min(e // 2, nx - e // 2), -(e % 2)))
    partner = (b, r + 1 - 2 * c)
    near = b + 1 - 2 * yl
    same = (near, r)
    other = (near, r + 2 - 4 * yh)

    def rating_load(s):
        return pltpu.make_async_copy(ratings_hbm.at[s], rbuf.at[s], load_sem.at[s])

    user_load = pltpu.make_async_copy(users_hbm, users, load_sem.at[3])
    item_load = pltpu.make_async_copy(items_hbm, block_0, load_sem.at[4])
    small = [(user_tiles_hbm, user_tiles), (item_tiles_hbm, item_tiles), (counts_hbm, counts)]
    small_loads = [
        pltpu.make_async_copy(src, dst, load_sem.at[5 + i]) for i, (src, dst) in enumerate(small)
    ]
    for load in small_loads:
        load.start()
    user_load.start()
    item_load.start()
    for s in ORDER:
        rating_load(s).start()

    barrier = pltpu.get_barrier_semaphore()
    friends = [partner, (col(-2), r), (col(2), r)]
    friends += [(col(s), 2 * target(e) + c) for s in (1, -1) for e in range(nq)]
    friends += [(b, 2 * target(e) + c) for e in range(1, nq)]
    friends += [(b, 2 * target(e) + 1 - c) for e in range(1, nq) if nx > 1 and e // 2 == nx // 2]
    for friend in friends:
        pl.semaphore_signal(barrier, inc=1, device_id=friend, device_id_type=MESH)
    zero = jnp.zeros((tile, tile), F32)
    for s in range(3):
        sums_user[s, slots] = zero
        sums_item[s, slots] = zero
    for load in small_loads:
        load.wait()
    picks = (user_tiles, item_tiles)
    for s in range(3):

        def link(k, seen, s=s):
            kept = []
            for side in range(2):
                mine = seen[side * tiles : (side + 1) * tiles]
                pick = picks[side][s, 0, k]
                before = slots
                for t in range(tiles):
                    before = jnp.where(pick == t, mine[t], before)
                    kept.append(jnp.where(pick == t, k, mine[t]))
                prev[s, side, k] = before
            return tuple(kept)

        seen = lax.fori_loop(0, slots, link, (jnp.int32(slots),) * (2 * tiles))
        for side in range(2):
            for t in range(tiles):
                last[s, side, t] = seen[side * tiles + t]
    pl.semaphore_wait(barrier, len(friends))

    def remote(src, dst, sems, i, target):
        return pltpu.make_async_remote_copy(
            src_ref=src,
            dst_ref=dst,
            send_sem=sems.at[0, i],
            recv_sem=sems.at[1, i],
            device_id=target,
            device_id_type=MESH,
        )

    def part(h):
        return pl.ds((2 * c + h) * quarter, quarter)

    def far_copy(h):
        return remote(items_hbm.at[part(h)], block_2.at[part(h)], fetch_sem, h, (col(-2), r))

    def near_copy(h, src):
        return remote(src, block_1.at[part(h)], fetch_sem, 2 + h, other if h else same)

    def swap_copy(s, h):
        view = blocks[s].at[part(h)]
        return remote(view, view, swap_sem, 2 * (s - 1) + h, partner)

    for h in range(2):
        far_copy(h).start()

    @pl.when(yl == 1)
    def _():
        for h in range(2):
            near_copy(h, items_hbm.at[part(h)]).start()

    def compute(s):
        for t in range(tiles):
            flipped[t] = blocks[s][t].T
        count = counts[0, 0, s]

        def body(i, carry):
            base = i * GROUP
            held = []
            for g in range(GROUP):
                k = base + g
                u = users[user_tiles[s, 0, k]]
                it = item_tiles[s, 0, k]
                v = blocks[s][it]
                p = jnp.dot(u, flipped[it], preferred_element_type=F32)
                rating = rbuf[s, k].astype(F32)
                live = (k < count).astype(F32)
                e = ((1.0 + CONFIDENCE * rating) * (rating - p) * live).astype(BF16)
                held.append((k, u, v, e))
            for k, u, v, e in held:
                gu = jnp.dot(e, v, preferred_element_type=F32)
                gi = lax.dot_general(e, u, (((0,), (0,)), ((), ())), preferred_element_type=F32)
                sums_user[s, k] = gu + sums_user[s, prev[s, 0, k]]
                sums_item[s, k] = gi + sums_item[s, prev[s, 1, k]]
            return carry

        lax.fori_loop(0, slots // GROUP, body, 0)

    def half_copy(s):
        return remote(half_out.at[s], half_in.at[s], half_sem, s, partner)

    def send_half(s):
        for t in range(tiles):
            end = last[s, 1, t]
            rows = pl.ds(pl.multiple_of((1 - c) * half, half), half)
            half_out[s, t] = sums_item[s, end, rows].astype(BF16)
        half_copy(s).start()

    def piece_copy(s, e):
        return remote(
            chip_sum.at[s, pl.ds(target(e) * per, per)],
            pieces.at[s, e],
            piece_sem,
            s * nq + e,
            (col(1) if s == 1 else b, 2 * target(e) + c),
        )

    def outgoing(s):
        return by_distance + [0] if s == 1 else by_distance

    def send_pieces(s):
        half_copy(s).wait_recv()
        for t in range(tiles):
            end = last[s, 1, t]
            rows = pl.ds(pl.multiple_of(c * half, half), half)
            both = sums_item[s, end, rows] + half_in[s, t].astype(F32)
            chip_sum[s, t] = both.astype(BF16)
        for e in outgoing(s):
            piece_copy(s, e).start()

    def column_sum(s):
        for e in outgoing(s):
            piece_copy(s, e).wait_recv()
        total = None if s == 1 else chip_sum[s, pl.ds(q * per, per)].astype(F32)
        for e in outgoing(s):
            term = pieces[s, e].astype(F32)
            total = term if total is None else total + term
        return total

    def fwd_copy(s):
        return remote(fwd_out, fwd_in, fwd_sem, 0, (col(s), r))

    user_load.wait()
    item_load.wait()
    rating_load(0).wait()
    compute(0)
    send_half(0)

    for h in range(2):
        far_copy(h).wait_recv()
        swap_copy(2, h).start()

        @pl.when(yl == 0)
        def _():
            near_copy(h, block_2.at[part(h)]).start()

    send_pieces(0)
    for h in range(2):
        swap_copy(2, h).wait_recv()
    rating_load(2).wait()
    compute(2)
    send_half(2)

    for h in range(2):
        near_copy(h, items_hbm.at[part(h)]).wait_recv()
        swap_copy(1, h).start()
    send_pieces(2)
    for h in range(2):
        swap_copy(1, h).wait_recv()
    rating_load(1).wait()
    compute(1)
    send_half(1)

    for t in range(tiles):
        grad = zero
        for s in ORDER:
            grad = grad + sums_user[s, last[s, 0, t]]
        old = users[t].astype(F32)
        unew[t] = (old - rate_user * (grad + SHRINKAGE * old)).astype(BF16)
    user_store = pltpu.make_async_copy(unew, user_out, out_sem.at[0])
    user_store.start()

    send_pieces(1)
    fwd_out[...] = column_sum(2)
    fwd_copy(2).start()
    total = column_sum(0)
    fwd_copy(2).wait_recv()
    total = total + fwd_in[...]
    total = total + column_sum(1)

    mine = pl.ds(q * per, per)
    old = block_0[mine, pl.ds(pl.multiple_of(c * half, half), half)].astype(F32)
    inew[mine, c] = (old - rate_item * (total + SHRINKAGE * old)).astype(BF16)

    farthest = [e for e in range(1, nq) if nx > 1 and e // 2 == nx // 2]
    nearer = [e for e in reversed(by_distance) if e not in farthest]

    def gather_copy(e, cross=0):
        view = inew.at[mine, c]
        core = 1 - c if cross else c
        return remote(view, view, gather_sem, cross * nq + e, (b, 2 * target(e) + core))

    def gathered(e, cross=0):
        core = 1 - c if cross else c
        view = inew.at[pl.ds(source(e) * per, per), core]
        return remote(view, view, gather_sem, cross * nq + e, (b, 2 * target(e) + core))

    def pair_copy(e):
        view = inew.at[pl.ds(source(e) * per, per), c]
        return remote(view, view, pair_sem, e, partner)

    def paired(e):
        view = inew.at[pl.ds(source(e) * per, per), 1 - c]
        return remote(view, view, pair_sem, e, partner)

    for e in farthest:
        gather_copy(e).start()
        gather_copy(e, 1).start()
    for e in reversed(nearer):
        gather_copy(e).start()
    pair_copy(0).start()
    for e in nearer:
        gathered(e).wait_recv()
        pair_copy(e).start()
    for e in [0] + nearer:
        paired(e).wait_recv()
    for e in farthest:
        gathered(e).wait_recv()
        gathered(e, 1).wait_recv()
    item_store = pltpu.make_async_copy(inew, item_out, out_sem.at[1])
    item_store.start()

    for h in range(2):
        far_copy(h).wait_send()
        near_copy(h, items_hbm.at[part(h)]).wait_send()
        for s in (1, 2):
            swap_copy(s, h).wait_send()
    for s in ORDER:
        half_copy(s).wait_send()
        for e in outgoing(s):
            piece_copy(s, e).wait_send()
    fwd_copy(2).wait_send()
    for e in farthest:
        gather_copy(e).wait_send()
        gather_copy(e, 1).wait_send()
    for e in nearer:
        gather_copy(e).wait_send()
    for e in [0] + nearer:
        pair_copy(e).wait_send()
    user_store.wait()
    item_store.wait()


def finish(user_raw, item_raw, user_out, item_out, user_buf, item_buf, sem):
    moves = []
    for a, (src, buf, dst) in enumerate(
        ((user_raw, user_buf, user_out), (item_raw, item_buf, item_out))
    ):
        for p in range(2):
            rows = pl.ds(p * (buf.shape[0] // 2), buf.shape[0] // 2)
            i = 2 * a + p
            into = pltpu.make_async_copy(src.at[rows], buf.at[rows], sem.at[0, i])
            away = pltpu.make_async_copy(buf.at[rows], dst.at[rows], sem.at[1, i])
            into.start()
            moves.append((into, away))
    for into, away in moves:
        into.wait()
        away.start()
    for _, away in moves:
        away.wait()


def on_device(users, items, ratings, user_tiles, item_tiles, counts):
    tile = ratings.shape[-1]
    rank = users.shape[1]
    stops, slots = ratings.shape[2:4]
    tiles = users.shape[0] // tile
    half = tile // 2
    nq = lax.axis_size("rep") // 2
    per = tiles // nq
    rate_user = STEP_GAIN / math.sqrt(stops * slots * tile * tile / users.shape[0])
    rate_item = STEP_GAIN / math.sqrt(2 * nq * stops * slots * tile * tile / items.shape[0])
    hbm = pl.BlockSpec(memory_space=pltpu.HBM)
    anywhere = pl.BlockSpec(memory_space=pl.ANY)
    dma = pltpu.SemaphoreType.DMA
    user_new, item_new = pl.pallas_call(
        functools.partial(kernel, rate_user, rate_item),
        out_shape=(
            jax.ShapeDtypeStruct((tiles, tile, rank), BF16),
            jax.ShapeDtypeStruct((tiles, 2, half, rank), BF16),
        ),
        in_specs=[hbm] * 6,
        out_specs=(anywhere, anywhere),
        scratch_shapes=[
            pltpu.VMEM((tiles, tile, rank), BF16),
            pltpu.VMEM((tiles, tile, rank), BF16),
            pltpu.VMEM((tiles, tile, rank), BF16),
            pltpu.VMEM((tiles, tile, rank), BF16),
            pltpu.VMEM((tiles, rank, tile), BF16),
            pltpu.VMEM((stops, slots, tile, tile), BF16),
            pltpu.VMEM((stops, slots + 1, tile, rank), F32),
            pltpu.VMEM((stops, slots + 1, tile, rank), F32),
            pltpu.VMEM((stops, tiles, half, rank), BF16),
            pltpu.VMEM((stops, tiles, half, rank), BF16),
            pltpu.VMEM((stops, tiles, half, rank), BF16),
            pltpu.VMEM((stops, nq, per, half, rank), BF16),
            pltpu.VMEM((per, half, rank), F32),
            pltpu.VMEM((per, half, rank), F32),
            pltpu.VMEM((tiles, tile, rank), BF16),
            pltpu.VMEM((tiles, 2, half, rank), BF16),
            pltpu.SMEM((stops, 1, slots), jnp.int32),
            pltpu.SMEM((stops, 1, slots), jnp.int32),
            pltpu.SMEM((1, 1, stops), jnp.int32),
            pltpu.SMEM((stops, 2, slots), jnp.int32),
            pltpu.SMEM((stops, 2, tiles), jnp.int32),
            dma((8,)),
            dma((2, 4)),
            dma((2, 4)),
            dma((2, 3)),
            dma((2, 3 * nq)),
            dma((2, 1)),
            dma((2, 2 * nq)),
            dma((2, nq)),
            dma((2,)),
        ],
        compiler_params=pltpu.CompilerParams(
            collective_id=0, has_side_effects=True, vmem_limit_bytes=67043328
        ),
    )(
        user_tiles.reshape(stops, 1, slots),
        item_tiles.reshape(stops, 1, slots),
        counts,
        users.reshape(tiles, tile, rank),
        items.reshape(tiles, tile, rank),
        ratings[0, 0],
    )
    user_new = user_new.reshape(users.shape)
    item_new = item_new.reshape(items.shape)
    return pl.pallas_call(
        finish,
        out_shape=(
            jax.ShapeDtypeStruct(users.shape, BF16),
            jax.ShapeDtypeStruct(items.shape, BF16),
        ),
        in_specs=[anywhere, anywhere],
        out_specs=(anywhere, anywhere),
        scratch_shapes=[pltpu.VMEM(users.shape, BF16), pltpu.VMEM(items.shape, BF16), dma((2, 4))],
    )(user_new, item_new)


def solution(mesh):
    return jax.shard_map(
        on_device,
        mesh=mesh,
        in_specs=(
            P(("blk", "rep"), None),
            P("blk", None),
            P("blk", "rep", None, None, None, None),
            P("blk", "rep", None, None),
            P("blk", "rep", None, None),
            P("blk", "rep", None),
        ),
        out_specs=(P(("blk", "rep"), None), P("blk", None)),
        check_vma=False,
    )
```

time: 53.8 us -> 46.2 us (0.86)
  local copies, waits for them, and re-layouts: 4.07 us -> 0 us
  other arithmetic: 3.63 us -> 0 us
    unnamed x2 -> x0, local copies, waits for them, and re-layouts: 3.34 us -> none
    concatenate x2 -> x0, other arithmetic: 2.13 us -> none  [the longest x1 1.36 us: slot_table(): return jnp.concatenate([picks, found, tail], axis=2)]
    pallas_call x0 -> x1, Pallas kernels: none -> 1.82 us  [on_device(): pl.pallas_call(finish, out_shape=(jax.ShapeDtypeStruct(users.shape, BF16)...]
    pallas_call x1, Pallas kernels: 45.1 us -> 43.6 us  [on_device(): pl.pallas_call(functools.partial(kernel, rate_user, rate_item), out_shape...]
    broadcast_in_dim x2 -> x0, local copies, waits for them, and re-layouts: 0.73 us -> none  [the longest x1 0.72 us: slot_table(): tail = jnp.broadcast_to(counts[:, None, None], (stops, 2, 1))]
    another operation x1 -> x0, other arithmetic: 0.71 us -> none  [slot_table(): picks = jnp.stack([user_tiles, item_tiles], axis=1)]
    lt x1 -> x0, other arithmetic: 0.66 us -> none  [slot_table(): ids[None, :] < limit[:, None]]
where the time goes in v2:
time: 46.2 us; the launch traced here: 46.1 us
  Pallas kernels  45.4 us (98%)
  between operations  0.64 us (1%)
    pallas_call x1, Pallas kernels, on_device(): pl.pallas_call(functools.partial(kernel, rate_user, rate_item), out_shape...  43.6 us
    pallas_call x1, Pallas kernels, on_device(): pl.pallas_call(finish, out_shape=(jax.ShapeDtypeStruct(users.shape, BF16)...  1.82 us

profile of v2, /device:TPU:1, one launch (start us, length us, event | category | flops | bytes accessed | tf_op | source)
XLA Modules:
  0.0 46.1 jit_solution(15742486249184542166)
XLA Ops:
  0.6 43.6 %shard_map.77 = (bf16[8,128,128]{2,1,0:T(8,128)(2,1)}, bf16[8,2,64,128]{3,2,1,0:T(8,128)(2,1)}) custom-call(s32[3,1,40]{2,1,0:T(1,128)} %bitcast.12, s32[3,1,40]{2,1,0:T(1,128)} %bitcast.13, s32[1,1,3]{2,1,0:T(1,128)} %counts_hbm.1, bf16[8,128,128]{2,1,0:T(8,128)(2,1)} %bitcast.8, bf16[8,128,128]{2,1,0:T(8,128)(2,1)} %bitcast.9, ...), custom_call_target="tpu_custom_call" | custom-call | tf_op jit(solution)/shard_map/pallas_call | solution.py:391
  44.3 1.8 %shard_map.78 = (bf16[1024,128]{1,0:T(8,128)(2,1)}, bf16[1024,128]{1,0:T(8,128)(2,1)}) custom-call(bf16[1024,128]{1,0:T(8,128)(2,1)} %bitcast.10, bf16[1024,128]{1,0:T(8,128)(2,1)} %bitcast.11), custom_call_target="tpu_custom_call" | custom-call | tf_op jit(solution)/shard_map/pallas_call | solution.py:444

commit v3 on v2

--- a/solution.py
+++ b/solution.py
@@ -48,8 +48,10 @@
     user_tiles,
     item_tiles,
     counts,
-    prev,
-    last,
+    tile_rows,
+    picks,
+    links,
+    table,
     load_sem,
     fetch_sem,
     swap_sem,
@@ -98,7 +100,13 @@
 
     user_load = pltpu.make_async_copy(users_hbm, users, load_sem.at[3])
     item_load = pltpu.make_async_copy(items_hbm, block_0, load_sem.at[4])
-    small = [(user_tiles_hbm, user_tiles), (item_tiles_hbm, item_tiles), (counts_hbm, counts)]
+    small = [
+        (user_tiles_hbm, tile_rows.at[0]),
+        (item_tiles_hbm, tile_rows.at[1]),
+        (user_tiles_hbm, user_tiles),
+        (item_tiles_hbm, item_tiles),
+        (counts_hbm, counts),
+    ]
     small_loads = [
         pltpu.make_async_copy(src, dst, load_sem.at[5 + i]) for i, (src, dst) in enumerate(small)
     ]
@@ -117,30 +125,6 @@
     for friend in friends:
         pl.semaphore_signal(barrier, inc=1, device_id=friend, device_id_type=MESH)
     zero = jnp.zeros((tile, tile), F32)
-    for s in range(3):
-        sums_user[s, slots] = zero
-        sums_item[s, slots] = zero
-    for load in small_loads:
-        load.wait()
-    picks = (user_tiles, item_tiles)
-    for s in range(3):
-
-        def link(k, seen, s=s):
-            kept = []
-            for side in range(2):
-                mine = seen[side * tiles : (side + 1) * tiles]
-                pick = picks[side][s, 0, k]
-                before = slots
-                for t in range(tiles):
-                    before = jnp.where(pick == t, mine[t], before)
-                    kept.append(jnp.where(pick == t, k, mine[t]))
-                prev[s, side, k] = before
-            return tuple(kept)
-
-        seen = lax.fori_loop(0, slots, link, (jnp.int32(slots),) * (2 * tiles))
-        for side in range(2):
-            for t in range(tiles):
-                last[s, side, t] = seen[side * tiles + t]
     pl.semaphore_wait(barrier, len(friends))
 
     def remote(src, dst, sems, i, target):
@@ -173,6 +157,28 @@
     def _():
         for h in range(2):
             near_copy(h, items_hbm.at[part(h)]).start()
+
+    for load in small_loads[:2]:
+        load.wait()
+    lane = lax.broadcasted_iota(jnp.int32, picks.shape, 1)
+    picks[...] = lane - slots
+    for side in range(2):
+        for s in range(3):
+            picks[pl.ds(3 * side + s, 1), pl.ds(0, slots)] = tile_rows[side, s]
+    wanted = picks[...]
+    found = jnp.full_like(wanted, slots)
+    for k in range(slots):
+        hit = (wanted == jnp.broadcast_to(wanted[:, k : k + 1], wanted.shape)) & (lane > k)
+        found = jnp.where(hit, k, found)
+    links[...] = found
+    table_copy = pltpu.make_async_copy(links, table, load_sem.at[10])
+    table_copy.start()
+    for s in range(3):
+        sums_user[s, slots] = zero
+        sums_item[s, slots] = zero
+    for load in small_loads[2:]:
+        load.wait()
+    table_copy.wait()
 
     def compute(s):
         for t in range(tiles):
@@ -195,8 +201,8 @@
             for k, u, v, e in held:
                 gu = jnp.dot(e, v, preferred_element_type=F32)
                 gi = lax.dot_general(e, u, (((0,), (0,)), ((), ())), preferred_element_type=F32)
-                sums_user[s, k] = gu + sums_user[s, prev[s, 0, k]]
-                sums_item[s, k] = gi + sums_item[s, prev[s, 1, k]]
+                sums_user[s, k] = gu + sums_user[s, table[s, k]]
+                sums_item[s, k] = gi + sums_item[s, table[3 + s, k]]
             return carry
 
         lax.fori_loop(0, slots // GROUP, body, 0)
@@ -206,7 +212,7 @@
 
     def send_half(s):
         for t in range(tiles):
-            end = last[s, 1, t]
+            end = table[3 + s, slots + t]
             rows = pl.ds(pl.multiple_of((1 - c) * half, half), half)
             half_out[s, t] = sums_item[s, end, rows].astype(BF16)
         half_copy(s).start()
@@ -226,7 +232,7 @@
     def send_pieces(s):
         half_copy(s).wait_recv()
         for t in range(tiles):
-            end = last[s, 1, t]
+            end = table[3 + s, slots + t]
             rows = pl.ds(pl.multiple_of(c * half, half), half)
             both = sums_item[s, end, rows] + half_in[s, t].astype(F32)
             chip_sum[s, t] = both.astype(BF16)
@@ -279,7 +285,7 @@
     for t in range(tiles):
         grad = zero
         for s in ORDER:
-            grad = grad + sums_user[s, last[s, 0, t]]
+            grad = grad + sums_user[s, table[s, slots + t]]
         old = users[t].astype(F32)
         unew[t] = (old - rate_user * (grad + SHRINKAGE * old)).astype(BF16)
     user_store = pltpu.make_async_copy(unew, user_out, out_sem.at[0])
@@ -416,9 +422,11 @@
             pltpu.SMEM((stops, 1, slots), jnp.int32),
             pltpu.SMEM((stops, 1, slots), jnp.int32),
             pltpu.SMEM((1, 1, stops), jnp.int32),
-            pltpu.SMEM((stops, 2, slots), jnp.int32),
-            pltpu.SMEM((stops, 2, tiles), jnp.int32),
-            dma((8,)),
+            pltpu.VMEM((2, stops, 1, slots), jnp.int32),
+            pltpu.VMEM((8, 128), jnp.int32),
+            pltpu.VMEM((8, 128), jnp.int32),
+            pltpu.SMEM((8, 128), jnp.int32),
+            dma((11,)),
             dma((2, 4)),
             dma((2, 4)),
             dma((2, 3)),

time: 46.2 us -> 46 us (level)
  no operation moved by 1% of the time
where the time goes in v3:
time: 46 us; the launch traced here: 45.8 us
  Pallas kernels  45.2 us (98%)
  between operations  0.64 us (1%)
    pallas_call x1, Pallas kernels, on_device(): pl.pallas_call(functools.partial(kernel, rate_user, rate_item), out_shape...  43.4 us
    pallas_call x1, Pallas kernels, on_device(): pl.pallas_call(finish, out_shape=(jax.ShapeDtypeStruct(users.shape, BF16)...  1.82 us

profile of v3, /device:TPU:1, one launch (start us, length us, event | category | flops | bytes accessed | tf_op | source)
XLA Modules:
  0.0 45.8 jit_solution(11802287143996739381)
XLA Ops:
  0.6 43.4 %shard_map.77 = (bf16[8,128,128]{2,1,0:T(8,128)(2,1)}, bf16[8,2,64,128]{3,2,1,0:T(8,128)(2,1)}) custom-call(s32[3,1,40]{2,1,0:T(1,128)} %bitcast.12, s32[3,1,40]{2,1,0:T(1,128)} %bitcast.13, s32[1,1,3]{2,1,0:T(1,128)} %counts_hbm.1, bf16[8,128,128]{2,1,0:T(8,128)(2,1)} %bitcast.8, bf16[8,128,128]{2,1,0:T(8,128)(2,1)} %bitcast.9, ...), custom_call_target="tpu_custom_call" | custom-call | tf_op jit(solution)/shard_map/pallas_call | solution.py:397
  44.0 1.8 %shard_map.78 = (bf16[1024,128]{1,0:T(8,128)(2,1)}, bf16[1024,128]{1,0:T(8,128)(2,1)}) custom-call(bf16[1024,128]{1,0:T(8,128)(2,1)} %bitcast.10, bf16[1024,128]{1,0:T(8,128)(2,1)} %bitcast.11), custom_call_target="tpu_custom_call" | custom-call | tf_op jit(solution)/shard_map/pallas_call | solution.py:452

commit v4 on v3

--- a/solution.py
+++ b/solution.py
@@ -59,7 +59,6 @@
     piece_sem,
     fwd_sem,
     gather_sem,
-    pair_sem,
     out_sem,
 ):
     blocks = (block_0, block_1, block_2)
@@ -121,7 +120,7 @@
     friends = [partner, (col(-2), r), (col(2), r)]
     friends += [(col(s), 2 * target(e) + c) for s in (1, -1) for e in range(nq)]
     friends += [(b, 2 * target(e) + c) for e in range(1, nq)]
-    friends += [(b, 2 * target(e) + 1 - c) for e in range(1, nq) if nx > 1 and e // 2 == nx // 2]
+    friends += [(b, 2 * target(e) + 1 - c) for e in range(1, nq)]
     for friend in friends:
         pl.semaphore_signal(barrier, inc=1, device_id=friend, device_id_type=MESH)
     zero = jnp.zeros((tile, tile), F32)
@@ -303,9 +302,6 @@
     old = block_0[mine, pl.ds(pl.multiple_of(c * half, half), half)].astype(F32)
     inew[mine, c] = (old - rate_item * (total + SHRINKAGE * old)).astype(BF16)
 
-    farthest = [e for e in range(1, nq) if nx > 1 and e // 2 == nx // 2]
-    nearer = [e for e in reversed(by_distance) if e not in farthest]
-
     def gather_copy(e, cross=0):
         view = inew.at[mine, c]
         core = 1 - c if cross else c
@@ -316,28 +312,11 @@
         view = inew.at[pl.ds(source(e) * per, per), core]
         return remote(view, view, gather_sem, cross * nq + e, (b, 2 * target(e) + core))
 
-    def pair_copy(e):
-        view = inew.at[pl.ds(source(e) * per, per), c]
-        return remote(view, view, pair_sem, e, partner)
-
-    def paired(e):
-        view = inew.at[pl.ds(source(e) * per, per), 1 - c]
-        return remote(view, view, pair_sem, e, partner)
-
-    for e in farthest:
-        gather_copy(e).start()
-        gather_copy(e, 1).start()
-    for e in reversed(nearer):
-        gather_copy(e).start()
-    pair_copy(0).start()
-    for e in nearer:
-        gathered(e).wait_recv()
-        pair_copy(e).start()
-    for e in [0] + nearer:
-        paired(e).wait_recv()
-    for e in farthest:
-        gathered(e).wait_recv()
-        gathered(e, 1).wait_recv()
+    gathers = [(e, cross) for e in by_distance for cross in (0, 1)] + [(0, 1)]
+    for e, cross in gathers:
+        gather_copy(e, cross).start()
+    for e, cross in reversed(gathers):
+        gathered(e, cross).wait_recv()
     item_store = pltpu.make_async_copy(inew, item_out, out_sem.at[1])
     item_store.start()
 
@@ -351,34 +330,21 @@
         for e in outgoing(s):
             piece_copy(s, e).wait_send()
     fwd_copy(2).wait_send()
-    for e in farthest:
-        gather_copy(e).wait_send()
-        gather_copy(e, 1).wait_send()
-    for e in nearer:
-        gather_copy(e).wait_send()
-    for e in [0] + nearer:
-        pair_copy(e).wait_send()
+    for e, cross in gathers:
+        gather_copy(e, cross).wait_send()
     user_store.wait()
     item_store.wait()
 
 
-def finish(user_raw, item_raw, user_out, item_out, user_buf, item_buf, sem):
-    moves = []
-    for a, (src, buf, dst) in enumerate(
-        ((user_raw, user_buf, user_out), (item_raw, item_buf, item_out))
-    ):
-        for p in range(2):
-            rows = pl.ds(p * (buf.shape[0] // 2), buf.shape[0] // 2)
-            i = 2 * a + p
-            into = pltpu.make_async_copy(src.at[rows], buf.at[rows], sem.at[0, i])
-            away = pltpu.make_async_copy(buf.at[rows], dst.at[rows], sem.at[1, i])
-            into.start()
-            moves.append((into, away))
-    for into, away in moves:
-        into.wait()
-        away.start()
-    for _, away in moves:
-        away.wait()
+def finish(user_new, item_new, user_out, item_out, sem):
+    moves = [
+        pltpu.make_async_copy(user_new, user_out, sem.at[0]),
+        pltpu.make_async_copy(item_new, item_out, sem.at[1]),
+    ]
+    for move in moves:
+        move.start()
+    for move in moves:
+        move.wait()
 
 
 def on_device(users, items, ratings, user_tiles, item_tiles, counts):
@@ -397,8 +363,8 @@
     user_new, item_new = pl.pallas_call(
         functools.partial(kernel, rate_user, rate_item),
         out_shape=(
-            jax.ShapeDtypeStruct((tiles, tile, rank), BF16),
-            jax.ShapeDtypeStruct((tiles, 2, half, rank), BF16),
+            pltpu.VMEM((tiles, tile, rank), BF16),
+            pltpu.VMEM((tiles, 2, half, rank), BF16),
         ),
         in_specs=[hbm] * 6,
         out_specs=(anywhere, anywhere),
@@ -433,11 +399,10 @@
             dma((2, 3 * nq)),
             dma((2, 1)),
             dma((2, 2 * nq)),
-            dma((2, nq)),
             dma((2,)),
         ],
         compiler_params=pltpu.CompilerParams(
-            collective_id=0, has_side_effects=True, vmem_limit_bytes=67043328
+            collective_id=0, has_side_effects=True, vmem_limit_bytes=60000000
         ),
     )(
         user_tiles.reshape(stops, 1, slots),
@@ -455,9 +420,10 @@
             jax.ShapeDtypeStruct(users.shape, BF16),
             jax.ShapeDtypeStruct(items.shape, BF16),
         ),
-        in_specs=[anywhere, anywhere],
+        in_specs=[pl.BlockSpec(memory_space=pltpu.VMEM)] * 2,
         out_specs=(anywhere, anywhere),
-        scratch_shapes=[pltpu.VMEM(users.shape, BF16), pltpu.VMEM(items.shape, BF16), dma((2, 4))],
+        scratch_shapes=[dma((2,))],
+        compiler_params=pltpu.CompilerParams(vmem_limit_bytes=4 << 20),
     )(user_new, item_new)
 
 

time: 46 us -> 43.1 us (0.937)
  Pallas kernels: 45.2 us -> 42.4 us
    pallas_call x1, Pallas kernels: 43.4 us -> 41.6 us  [on_device(): pl.pallas_call(functools.partial(kernel, rate_user, rate_item), out_shape...]
    pallas_call x1, Pallas kernels: 1.82 us -> 0.81 us  [on_device(): pl.pallas_call(finish, out_shape=(jax.ShapeDtypeStruct(users.shape, BF16)...]
where the time goes in v4:
time: 43.1 us; the launch traced here: 43 us
  Pallas kernels  42.4 us (98%)
  between operations  0.64 us (1%)
    pallas_call x1, Pallas kernels, on_device(): pl.pallas_call(functools.partial(kernel, rate_user, rate_item), out_shape...  41.6 us

profile of v4, /device:TPU:1, one launch (start us, length us, event | category | flops | bytes accessed | tf_op | source)
XLA Modules:
  0.0 43.0 jit_solution(13526580797551963514)
XLA Ops:
  0.6 41.6 %shard_map.77 = (bf16[8,128,128]{2,1,0:T(8,128)(2,1)S(1)}, bf16[8,2,64,128]{3,2,1,0:T(8,128)(2,1)S(1)}) custom-call(s32[3,1,40]{2,1,0:T(1,128)} %bitcast.12, s32[3,1,40]{2,1,0:T(1,128)} %bitcast.13, s32[1,1,3]{2,1,0:T(1,128)} %counts_hbm.1, bf16[8,128,128]{2,1,0:T(8,128)(2,1)} %bitcast.10, bf16[8,128,128]{2,1,0:T(8,128)(2,1)} %bitcast.11, ...), custom_call_target="tpu_custom_call" | custom-call | tf_op jit(solution)/shard_map/pallas_call | solution.py:363
  42.2 0.8 %shard_map.78 = (bf16[1024,128]{1,0:T(8,128)(2,1)}, bf16[1024,128]{1,0:T(8,128)(2,1)}) custom-call(bf16[1024,128]{1,0:T(8,128)(2,1)S(1)} %bitcast.7, bf16[1024,128]{1,0:T(8,128)(2,1)S(1)} %bitcast.8), custom_call_target="tpu_custom_call" | custom-call | tf_op jit(solution)/shard_map/pallas_call | solution.py:417

commit v5 on v4

--- a/solution.py
+++ b/solution.py
@@ -11,7 +11,7 @@
 CONFIDENCE = 0.5
 SHRINKAGE = 0.05
 STEP_GAIN = 0.3
-GROUP = 20
+GROUP = 40
 MESH = pl.DeviceIdType.MESH
 F32 = jnp.float32
 BF16 = jnp.bfloat16
@@ -230,13 +230,15 @@
 
     def send_pieces(s):
         half_copy(s).wait_recv()
-        for t in range(tiles):
-            end = table[3 + s, slots + t]
-            rows = pl.ds(pl.multiple_of(c * half, half), half)
-            both = sums_item[s, end, rows] + half_in[s, t].astype(F32)
-            chip_sum[s, t] = both.astype(BF16)
-        for e in outgoing(s):
-            piece_copy(s, e).start()
+        for e in outgoing(s) + ([] if s == 1 else [0]):
+            for p in range(per):
+                t = target(e) * per + p
+                end = table[3 + s, slots + t]
+                rows = pl.ds(pl.multiple_of(c * half, half), half)
+                both = sums_item[s, end, rows] + half_in[s, t].astype(F32)
+                chip_sum[s, t] = both.astype(BF16)
+            if s == 1 or e > 0:
+                piece_copy(s, e).start()
 
     def column_sum(s):
         for e in outgoing(s):

time: 43.1 us -> 43.1 us (level)
  no operation moved by 1% of the time
where the time goes in v5:
time: 43.1 us; the launch traced here: 42.9 us
  Pallas kernels  42.3 us (98%)
  between operations  0.64 us (1%)
    pallas_call x1, Pallas kernels, on_device(): pl.pallas_call(functools.partial(kernel, rate_user, rate_item), out_shape...  41.5 us

profile of v5, /device:TPU:1, one launch (start us, length us, event | category | flops | bytes accessed | tf_op | source)
XLA Modules:
  0.0 42.9 jit_solution(14764147041567058860)
XLA Ops:
  0.6 41.5 %shard_map.77 = (bf16[8,128,128]{2,1,0:T(8,128)(2,1)S(1)}, bf16[8,2,64,128]{3,2,1,0:T(8,128)(2,1)S(1)}) custom-call(s32[3,1,40]{2,1,0:T(1,128)} %bitcast.12, s32[3,1,40]{2,1,0:T(1,128)} %bitcast.13, s32[1,1,3]{2,1,0:T(1,128)} %counts_hbm.1, bf16[8,128,128]{2,1,0:T(8,128)(2,1)} %bitcast.10, bf16[8,128,128]{2,1,0:T(8,128)(2,1)} %bitcast.11, ...), custom_call_target="tpu_custom_call" | custom-call | tf_op jit(solution)/shard_map/pallas_call | solution.py:365
  42.1 0.8 %shard_map.78 = (bf16[1024,128]{1,0:T(8,128)(2,1)}, bf16[1024,128]{1,0:T(8,128)(2,1)}) custom-call(bf16[1024,128]{1,0:T(8,128)(2,1)S(1)} %bitcast.7, bf16[1024,128]{1,0:T(8,128)(2,1)S(1)} %bitcast.8), custom_call_target="tpu_custom_call" | custom-call | tf_op jit(solution)/shard_map/pallas_call | solution.py:419
